TPU v7x, 256 devices: a whole 4x4x8 slice. The times are simulated.
256 devices in a mesh: order: 16 (over y, x), level: 8 (over z), freq: 2 (over core).
Axes of the slice: x: 4, y: 4, z: 8, core: 2. Of those that a mesh axis runs over, the one named last changes fastest.
Arguments:
- fourier: bfloat16 [64, 8, 8, 128, 512], P('freq', None, 'level', 'order'), parts along dimension 0, may hold values from -6 to 6
- order_slot: int32 [32], replicated, may hold values from 0 to 31, each once
- coeff_self: bfloat16 [6, 32, 64, 128, 128], P(None, 'order', 'level'), may hold values from -0.375 to 0.375
- coeff_pair: bfloat16 [6, 32, 64, 128, 128], P(None, 'order', 'level'), may hold values from -0.375 to 0.375
Outputs:
- butterfly: bfloat16 [64, 64, 128, 512], P(('freq', 'order'), 'level'), parts along dimension 0
There are 2 independent parts, one for each index of `freq`. A program takes and returns all parts, laid end to end along the dimension named above; an argument that names none is the same for every part. Nothing has to cross between parts.
Inputs may be any that keep to these rules, and one draw needn't show every extreme that they name: order_slot is a permutation of the orders.
All inputs are finite; a program needn't handle non-finite values.
Results may differ from a plain program's by a relative error of at most 0.008.
Values may be sent and summed in bfloat16 or wider, within the bound.
A program may use at most 64 MiB of HBM per device.

v0:
```python
import jax
import jax.numpy as jnp
from jax import lax
from jax.sharding import PartitionSpec as P


def partner_2(value, axis, stride):
    mask = 2**stride
    pairs = [(source, source ^ mask) for source in range(lax.axis_size(axis))]
    return lax.ppermute(value, axis, pairs)


def partner_blocks(values, height):
    extent = values.shape
    halves = values.reshape(
        extent[0], extent[1] >> height + 1, 2, 1 << height, extent[2], extent[3]
    )
    return halves[:, :, ::-1].reshape(extent)


def run_levels(current, factor_self, factor_pair):
    local_bits = current.shape[1].bit_length() - 1
    for height in range(factor_self.shape[0]):
        if height < local_bits:
            partner = partner_blocks(current, height)
        else:
            partner = partner_2(current, "level", height - local_bits)
        mixed_sum = jnp.einsum(
            "sbrq,sbqc->sbrc", factor_self[height], current, preferred_element_type=jnp.float32
        )
        mixed_sum = mixed_sum + jnp.einsum(
            "sbrq,sbqc->sbrc", factor_pair[height], partner, preferred_element_type=jnp.float32
        )
        current = mixed_sum.astype(jnp.bfloat16)
    return current


def local(fourier, order_slot, coeff_self, coeff_pair):
    picked = jnp.take(fourier, order_slot, axis=0)
    order_count = lax.axis_size("order")
    level_count = lax.axis_size("level")
    orders_here = coeff_self.shape[1]
    blocks_here = coeff_self.shape[2]
    cycle_rows = coeff_self.shape[3]
    rows_here = fourier.shape[3]
    columns = fourier.shape[4]
    group_size = blocks_here // level_count
    outgoing = picked.reshape(order_count, orders_here, level_count, group_size, rows_here, columns)
    outgoing = outgoing.transpose(0, 2, 1, 3, 4, 5).reshape(
        order_count * level_count * orders_here, group_size, 1, rows_here, columns
    )
    received = lax.all_to_all(outgoing, ("order", "level"), split_axis=0, concat_axis=2, tiled=True)
    received = received.reshape(
        orders_here, group_size, order_count, level_count, rows_here, columns
    )
    current = received.transpose(0, 1, 3, 2, 4, 5).reshape(
        orders_here, blocks_here, cycle_rows, columns
    )
    result = run_levels(current, coeff_self, coeff_pair)
    return result


def solution(mesh):
    placed = (
        P("freq", None, "level", "order", None),
        P(),
        P(None, "order", "level", None, None),
        P(None, "order", "level", None, None),
    )
    return jax.shard_map(
        local,
        mesh=mesh,
        in_specs=placed,
        out_specs=P(("freq", "order"), "level", None, None),
        check_vma=False,
    )
```

profile of v0, /device:TPU:1, one launch (start us, length us, event | category | flops | bytes accessed | tf_op | source)
XLA Modules:
  0.0 340.6 jit_solution(12960232268667124706)
XLA Ops:
  0.0 0.8 compare_and_fusion
  1.6 2.0 gather_fusion
  3.6 1.8 select_bitcast_fusion
  5.7 68.8 %all_to_all.15 = bf16[256,1,1,8,512]{4,3,2,1,0:T(8,128)(2,1)S(1)} all-to-all(bf16[256,1,1,8,512]{4,3,2,1,0:T(8,128)(2,1)S(1)} %bitcast.90), channel_id=1, replica_groups=mesh['order'=16,'level'=8,'freq'=2] {'order','level'}, dimensions={0} | all-to-all | bytes 4194304 | tf_op jit(solution)/shard_map/all_to_all | solution.py:52
  74.7 1.5 copy.29
  76.3 3.1 rev.9
  79.4 2.0 fusion
  81.4 2.0 add_convert_fusion.5
  83.4 3.7 %fusion.16 = f32[2,8,512,128]{3,2,1,0:T(8,128)} fusion(bf16[2,8,512,128]{3,2,1,0:T(8,128)(2,1)S(1)} %add_convert_fusion.5, bf16[6,2,8,128,128]{4,3,2,1,0:T(8,128)(2,1)} %param.6), kind=kOutput, calls=%fused_computation.24 | convolution fusion | flops 268435456 | bytes 6815744 | tf_op jit(solution)/shard_map/sbrq,sbqc->sbrc/dot_general | solution.py:28
  87.1 1.5 rev.10
  88.6 3.7 %add_convert_fusion.4 = bf16[2,8,512,128]{3,2,1,0:T(8,128)(2,1)S(1)} fusion(f32[2,8,512,128]{3,2,1,0:T(8,128)} %fusion.16, bf16[2,8,128,512]{2,3,1,0:T(8,128)(2,1)} %bitcast.87, bf16[6,2,8,128,128]{4,3,2,1,0:T(8,128)(2,1)} %param.7), kind=kOutput, calls=%fused_computation.5 | convolution fusion | flops 270532608 | bytes 8912896 | tf_op jit(solution)/shard_map/sbrq,sbqc->sbrc/dot_general | solution.py:31
  92.3 3.7 %fusion.13 = f32[2,8,512,128]{3,2,1,0:T(8,128)} fusion(bf16[2,8,512,128]{3,2,1,0:T(8,128)(2,1)S(1)} %add_convert_fusion.4, bf16[6,2,8,128,128]{4,3,2,1,0:T(8,128)(2,1)} %param.6), kind=kOutput, calls=%fused_computation.21 | convolution fusion | flops 268435456 | bytes 6815744 | tf_op jit(solution)/shard_map/sbrq,sbqc->sbrc/dot_general | solution.py:28
  96.0 1.5 rev.11
  97.5 3.8 %add_convert_fusion.3 = bf16[2,8,512,128]{3,2,1,0:T(8,128)(2,1)S(1)} fusion(f32[2,8,512,128]{3,2,1,0:T(8,128)} %fusion.13, bf16[2,8,128,512]{2,3,1,0:T(8,128)(2,1)} %bitcast.88, bf16[6,2,8,128,128]{4,3,2,1,0:T(8,128)(2,1)} %param.7), kind=kOutput, calls=%fused_computation.4 | convolution fusion | flops 270532608 | bytes 8912896 | tf_op jit(solution)/shard_map/sbrq,sbqc->sbrc/dot_general | solution.py:31
  101.9 0.7 fusion.10
  102.6 43.3 %collective-permute-done = bf16[2,8,128,512]{2,3,1,0:T(8,128)(2,1)S(1)} collective-permute-done((bf16[2,8,128,512]{2,3,1,0:T(8,128)(2,1)S(1)}, bf16[2,8,128,512]{2,3,1,0:T(8,128)(2,1)S(1)}, u32[]{:S(2)}, u32[]{:S(2)}) %collective-permute-start) | collective-permute-done | bytes 2097184 | tf_op jit(solution)/shard_map/ppermute | solution.py:10
  145.9 0.7 add_convert_fusion.2
  146.6 0.8 collective-permute-start.1
  148.1 91.6 %collective-permute-done.1 = bf16[2,8,128,512]{2,3,1,0:T(8,128)(2,1)S(1)} collective-permute-done((bf16[2,8,128,512]{2,3,1,0:T(8,128)(2,1)S(1)}, bf16[2,8,128,512]{2,3,1,0:T(8,128)(2,1)S(1)}, u32[]{:S(2)}, u32[]{:S(2)}) %collective-permute-start.1) | collective-permute-done | bytes 2097184 | tf_op jit(solution)/shard_map/ppermute | solution.py:10
  239.7 0.7 add_convert_fusion.1
  240.4 1.0 collective-permute-start.2
  242.1 92.5 %collective-permute-done.2 = bf16[2,8,128,512]{2,3,1,0:T(8,128)(2,1)S(1)} collective-permute-done((bf16[2,8,128,512]{2,3,1,0:T(8,128)(2,1)S(1)}, bf16[2,8,128,512]{2,3,1,0:T(8,128)(2,1)S(1)}, u32[]{:S(2)}, u32[]{:S(2)}) %collective-permute-start.2) | collective-permute-done | bytes 2097184 | tf_op jit(solution)/shard_map/ppermute | solution.py:10
  334.6 2.1 fusion.2
  336.7 3.9 %copy.33 = bf16[2,8,128,512]{3,2,1,0:T(8,128)(2,1)} copy(bf16[2,8,128,512]{2,3,1,0:T(8,128)(2,1)} %fusion.2) | data formatting | bytes 4194304 | tf_op jit(solution)/shard_map/convert_element_type | solution.py:34
  (18 shorter events, 3.2 us)
Async XLA Ops:
  0.0 1.6 copy-start
  79.4 2.0 copy-start.2
  97.5 4.4 %copy-start.4 = (bf16[6,2,8,128,128]{4,3,2,1,0:T(8,128)(2,1)S(1)}, bf16[6,2,8,128,128]{4,3,2,1,0:T(8,128)(2,1)}, u32[]{:S(2)}) copy-start(bf16[6,2,8,128,128]{4,3,2,1,0:T(8,128)(2,1)} %param.6) | copy-start | bytes 9437188
  101.3 44.6 %copy-start.3 = (bf16[6,2,8,128,128]{4,3,2,1,0:T(8,128)(2,1)S(1)}, bf16[6,2,8,128,128]{4,3,2,1,0:T(8,128)(2,1)}, u32[]{:S(2)}) copy-start(bf16[6,2,8,128,128]{4,3,2,1,0:T(8,128)(2,1)} %param.7) | copy-start | bytes 9437188
  101.3 44.6 %collective-permute-start = (bf16[2,8,128,512]{2,3,1,0:T(8,128)(2,1)S(1)}, bf16[2,8,128,512]{2,3,1,0:T(8,128)(2,1)S(1)}, u32[]{:S(2)}, u32[]{:S(2)}) collective-permute-start(bf16[2,8,128,512]{2,3,1,0:T(8,128)(2,1)S(1)} %bitcast.83), channel_id=1, source_target_pairs={{0,2},{2,0},{4,6},{6,4},{8,10},{10,8},{12,14},{14,12},{1,3},{3,1},... | collective-permute-start | bytes 6291464 | tf_op jit(solution)/shard_map/ppermute | solution.py:10
  146.6 93.1 %collective-permute-start.1 = (bf16[2,8,128,512]{2,3,1,0:T(8,128)(2,1)S(1)}, bf16[2,8,128,512]{2,3,1,0:T(8,128)(2,1)S(1)}, u32[]{:S(2)}, u32[]{:S(2)}) collective-permute-start(bf16[2,8,128,512]{2,3,1,0:T(8,128)(2,1)S(1)} %bitcast.84), channel_id=1, source_target_pairs={{0,4},{2,6},{4,0},{6,2},{8,12},{10,14},{12,8},{14,10},{1,5},{3,7},... | collective-permute-start | bytes 6291464 | tf_op jit(solution)/shard_map/ppermute | solution.py:10
  240.4 94.2 %collective-permute-start.2 = (bf16[2,8,128,512]{2,3,1,0:T(8,128)(2,1)S(1)}, bf16[2,8,128,512]{2,3,1,0:T(8,128)(2,1)S(1)}, u32[]{:S(2)}, u32[]{:S(2)}) collective-permute-start(bf16[2,8,128,512]{2,3,1,0:T(8,128)(2,1)S(1)} %bitcast.85), channel_id=1, source_target_pairs={{0,8},{2,10},{4,12},{6,14},{8,0},{10,2},{12,4},{14,6},{1,9},{3,11}... | collective-permute-start | bytes 6291464 | tf_op jit(solution)/shard_map/ppermute | solution.py:10
  334.6 6.0 %copy-start.1 = (bf16[32,8,1,8,512]{4,3,2,1,0:T(8,128)(2,1)S(1)}, bf16[32,8,1,8,512]{4,3,2,1,0:T(8,128)(2,1)}, u32[]{:S(2)}) copy-start(bf16[32,8,1,8,512]{4,3,2,1,0:T(8,128)(2,1)} %param.4) | copy-start | bytes 6291460
where the time goes:
time: 341 us
  waiting for transfers between devices  227 us (67%)
  blocking collectives  68.8 us (20%)
  matrix products  24.4 us (7%)
  local copies, waits for them, and re-layouts  14.2 us (4%)
    ppermute x3, waiting for transfers between devices, partner_2(): return lax.ppermute(value, axis, pairs)  227 us
    all_to_all x1, blocking collectives, local(): lax.all_to_all(outgoing, ('order', 'level'), split_axis=0, concat_axis=2,...  68.8 us
    dot_general x6, matrix products, run_levels(): jnp.einsum('sbrq,sbqc->sbrc', factor_pair[height], partner, preferred_ele...  13 us
    dot_general x6, matrix products, run_levels(): jnp.einsum('sbrq,sbqc->sbrc', factor_self[height], current, preferred_ele...  11.5 us
  transfers between devices with their start and end apart: 3, of which 3 were waited for; matrix products, arithmetic and copies ran while one was open for 1% of the time, Pallas kernels for 0%

commit v1 on v0

v1 whole, which is shorter than its diff:
```python
import functools

import jax
import jax.numpy as jnp
from jax import lax
from jax.experimental import pallas as pl
from jax.experimental.pallas import tpu as pltpu
from jax.sharding import PartitionSpec as P

MESH = pl.DeviceIdType.MESH
CHUNKS = 2


def mix(buf, c, coef, levels, slots, blocks):
    half = blocks // 2
    for k in range(levels):
        step = 1 << k

        def pair(i, carry, k=k, step=step):
            slot = lax.div(i, half)
            p = lax.rem(i, half)
            low = lax.div(p, step) * (2 * step) + lax.rem(p, step)
            high = low + step
            both = jnp.concatenate([buf[c, low, slot], buf[c, high, slot]], axis=0)
            top = jnp.concatenate([coef[0, k, slot, low], coef[1, k, slot, low]], axis=1)
            bottom = jnp.concatenate([coef[1, k, slot, high], coef[0, k, slot, high]], axis=1)
            rows = top.shape[0]
            mixed = jnp.dot(
                jnp.concatenate([top, bottom], axis=0), both, preferred_element_type=jnp.float32
            ).astype(jnp.bfloat16)
            buf[c, low, slot] = mixed[:rows]
            buf[c, high, slot] = mixed[rows:]
            return carry

        lax.fori_loop(0, slots * half, pair, 0)


def kernel(
    n_order, n_level, slot_ref, fourier_ref, self_ref, pair_ref, out_ref,
    cycles, stage, by_cycle, blocks, turned, near, far,
    load_sem, own_sem, z1_sem, xy_sem, z2_sem, z3_sem, coef_sem, core_sem,
):
    o, z, f = lax.axis_index("order"), lax.axis_index("level"), lax.axis_index("freq")
    chunks = stage.shape[0]
    orders, rows, width = stage.shape[2:]
    slots = orders // n_order
    levels = near.shape[1]
    other = 1 - f

    def at_level(d):
        return lax.rem(z + d, n_level)

    def at_order(d):
        return lax.rem(o + d, n_order)

    def loop(count, body):
        lax.fori_loop(1, count, lambda d, carry: (body(d), carry)[1], 0)

    loads = [
        pltpu.make_async_copy(fourier_ref, cycles, load_sem.at[0]),
        pltpu.make_async_copy(self_ref.at[pl.ds(0, levels)], near.at[0], load_sem.at[1]),
        pltpu.make_async_copy(pair_ref.at[pl.ds(0, levels)], near.at[1], load_sem.at[2]),
        pltpu.make_async_copy(self_ref.at[pl.ds(levels, levels), f, z], far.at[0, :, f, z], load_sem.at[3]),
        pltpu.make_async_copy(pair_ref.at[pl.ds(levels, levels), f, z], far.at[1, :, f, z], load_sem.at[4]),
    ]
    for copy in loads:
        copy.start()

    barrier = pltpu.get_barrier_semaphore()
    loop(n_level, lambda d: pl.semaphore_signal(barrier, 1, device_id=(o, at_level(d), f), device_id_type=MESH))
    loop(n_order, lambda d: pl.semaphore_signal(barrier, 1, device_id=(at_order(d), z, f), device_id_type=MESH))
    pl.semaphore_signal(barrier, 1, device_id=(o, z, other), device_id_type=MESH)
    pl.semaphore_wait(barrier, n_level + n_order - 1)

    def to_level(src, dst, sems, c, d):
        return pltpu.make_async_remote_copy(
            src, dst, sems.at[0, c, d], sems.at[1, c, d],
            device_id=(o, at_level(d), f), device_id_type=MESH,
        )

    def z1(c, d):
        return to_level(stage.at[c, at_level(d)], by_cycle.at[c, z], z1_sem, c, d)

    def xy(c, d):
        return pltpu.make_async_remote_copy(
            by_cycle.at[c, :, pl.ds(at_order(d) * slots, slots)],
            blocks.at[c, :, :, pl.ds(pl.multiple_of(o * rows, rows), rows)],
            xy_sem.at[0, c, d], xy_sem.at[1, c, d],
            device_id=(at_order(d), z, f), device_id_type=MESH,
        )

    def z2(c, d):
        return to_level(blocks.at[c, at_level(d)], turned.at[c, z], z2_sem, c, d)

    def z3(c, d):
        return to_level(
            turned.at[c, at_level(d)], out_ref.at[:, z, :, pl.ds(c * width, width)], z3_sem, c, d
        )

    def coef(which, d):
        src = (self_ref, pair_ref)[which]
        return to_level(
            src.at[pl.ds(levels, levels), f, at_level(d)], far.at[which, :, f, z], coef_sem, which, d
        )

    def core(which):
        return pltpu.make_async_remote_copy(
            far.at[which, :, f], far.at[which, :, f],
            core_sem.at[0, which], core_sem.at[1, which],
            device_id=(o, z, other), device_id_type=MESH,
        )

    own = {}
    for c in range(chunks):
        own["xy", c] = pltpu.make_async_copy(
            by_cycle.at[c, :, pl.ds(o * slots, slots)],
            blocks.at[c, :, :, pl.ds(pl.multiple_of(o * rows, rows), rows)],
            own_sem.at[0, c],
        )
        own["z2", c] = pltpu.make_async_copy(blocks.at[c, z], turned.at[c, z], own_sem.at[1, c])
        own["z3", c] = pltpu.make_async_copy(
            turned.at[c, z], out_ref.at[:, z, :, pl.ds(c * width, width)], own_sem.at[2, c]
        )

    loads[0].wait()
    for c in range(chunks):

        def place(s, carry, c=c):
            order = slot_ref[s]
            stage[c, :, s] = cycles[order, :, :, c * width : (c + 1) * width]
            by_cycle[c, z, s] = cycles[order, z, :, c * width : (c + 1) * width]
            return carry

        lax.fori_loop(0, orders, place, 0)
        loop(n_level, lambda d: z1(c, d).start())
    for which in range(2):
        loop(n_level, lambda d: coef(which, d).start())

    for copy in loads[1:]:
        copy.wait()
    for c in range(chunks):
        loop(n_level, lambda d: z1(c, d).wait_recv())
        loop(n_order, lambda d: xy(c, d).start())
        own["xy", c].start()
        own["xy", c].wait()
        loop(n_order, lambda d: xy(c, d).wait_recv())
        mix(blocks, c, near, levels, slots, n_level)
        loop(n_level, lambda d: z2(c, d).start())
        own["z2", c].start()

    for which in range(2):
        loop(n_level, lambda d: coef(which, d).wait_recv())
        core(which).start()
    for which in range(2):
        core(which).wait_recv()

    for c in range(chunks):
        own["z2", c].wait()
        loop(n_level, lambda d: z2(c, d).wait_recv())
        mix(turned, c, far, levels, slots, n_level)
        loop(n_level, lambda d: z3(c, d).start())
        own["z3", c].start()

    for which in range(2):
        loop(n_level, lambda d: coef(which, d).wait_send())
        core(which).wait_send()
    for c in range(chunks):
        loop(n_level, lambda d: z1(c, d).wait_send())
        loop(n_order, lambda d: xy(c, d).wait_send())
        loop(n_level, lambda d: z2(c, d).wait_send())
        own["z3", c].wait()
        loop(n_level, lambda d: z3(c, d).wait())


def local(n_order, n_level, fourier, order_slot, coeff_self, coeff_pair):
    orders, groups, _, rows, columns = fourier.shape
    all_levels, slots, blocks, cycle_rows, _ = coeff_self.shape
    levels = all_levels // 2
    width = columns // CHUNKS
    dtype = jnp.bfloat16
    hbm = pl.BlockSpec(memory_space=pl.ANY)
    coefs = pltpu.VMEM((2, levels, slots, blocks, cycle_rows, cycle_rows), dtype)
    spread = pltpu.VMEM((CHUNKS, n_level, orders, rows, width), dtype)
    whole = pltpu.VMEM((CHUNKS, n_level, slots, cycle_rows, width), dtype)
    dma = pltpu.SemaphoreType.DMA
    return pl.pallas_call(
        functools.partial(kernel, n_order, n_level),
        out_shape=jax.ShapeDtypeStruct((slots, blocks, cycle_rows, columns), dtype),
        in_specs=[pl.BlockSpec(memory_space=pltpu.SMEM), hbm, hbm, hbm],
        out_specs=hbm,
        scratch_shapes=[
            pltpu.VMEM((orders, groups, rows, columns), dtype),
            spread, spread, whole, whole, coefs, coefs,
            dma((5,)), dma((3, CHUNKS)),
            dma((2, CHUNKS, n_level)), dma((2, CHUNKS, n_order)),
            dma((2, CHUNKS, n_level)), dma((2, CHUNKS, n_level)),
            dma((2, 2, n_level)), dma((2, 2)),
        ],
        compiler_params=pltpu.CompilerParams(
            collective_id=0, has_side_effects=True, vmem_limit_bytes=40 << 20
        ),
        name="butterfly",
    )(order_slot, fourier.reshape(orders, groups, rows, columns), coeff_self, coeff_pair)


def solution(mesh):
    placed = (
        P("freq", None, "level", "order", None),
        P(),
        P(None, "order", "level", None, None),
        P(None, "order", "level", None, None),
    )
    return jax.shard_map(
        functools.partial(local, mesh.shape["order"], mesh.shape["level"]),
        mesh=mesh,
        in_specs=placed,
        out_specs=P(("freq", "order"), "level", None, None),
        check_vma=False,
    )
```

time: 341 us -> 192 us (0.56)
  waiting for transfers between devices: 227 us -> 0 us
  Pallas kernels: 0 us -> 181 us
  blocking collectives: 68.8 us -> 0 us
  matrix products: 24.4 us -> 0 us
  local copies, waits for them, and re-layouts: 14.2 us -> 7.34 us
    ppermute x3 -> x0, waiting for transfers between devices: 227 us -> none  [partner_2(): return lax.ppermute(value, axis, pairs)]
    pallas_call x0 -> x1, Pallas kernels: none -> 181 us  [local(): pl.pallas_call(functools.partial(kernel, n_order, n_level), out_shape=jax...]
    all_to_all x1 -> x0, blocking collectives: 68.8 us -> none  [local(): lax.all_to_all(outgoing, ('order', 'level'), split_axis=0, concat_axis=2,...]
    dot_general x12 -> x0, matrix products: 24.4 us -> none  [the longest x6 13 us: run_levels(): jnp.einsum('sbrq,sbqc->sbrc', factor_pair[height], partner, preferred_ele...]
    unnamed x10 -> x9, local copies, waits for them, and re-layouts: 0.05 us -> 7.34 us
    rev x3 -> x0, local copies, waits for them, and re-layouts: 6.15 us -> none  [partner_blocks(): return halves[:, :, ::-1].reshape(extent)]
    convert_element_type x1 -> x0, local copies, waits for them, and re-layouts: 3.94 us -> none  [run_levels(): current = mixed_sum.astype(jnp.bfloat16)]
  transfers between devices with their start and end apart: 3 -> 0, of which waited for: 3 -> 0; matrix products, arithmetic and copies ran while one was open for 1% -> 0% of each run, Pallas kernels for 0% -> 0%
where the time goes in v1:
time: 192 us; the launch traced here: 188 us
  Pallas kernels  181 us (94%)
  local copies, waits for them, and re-layouts  7.34 us (4%)
    pallas_call x1, Pallas kernels, local(): pl.pallas_call(functools.partial(kernel, n_order, n_level), out_shape=jax...  181 us
    unnamed x9, local copies, waits for them, and re-layouts  7.34 us

profile of v1, /device:TPU:1, one launch (start us, length us, event | category | flops | bytes accessed | tf_op | source)
XLA Modules:
  0.0 188.3 jit_solution(12241429249141976601)
XLA Ops:
  0.0 0.0 copy-start
  0.0 1.9 %copy-done = bf16[6,2,8,128,128]{4,3,2,1,0:T(8,128)(2,1)S(1)} copy-done((bf16[6,2,8,128,128]{4,3,2,1,0:T(8,128)(2,1)S(1)}, bf16[6,2,8,128,128]{4,3,2,1,0:T(8,128)(2,1)}, u32[]{:S(2)}) %copy-start) | copy-done | bytes 3145752
  1.9 0.0 copy-start.1
  1.9 1.9 %copy-done.1 = bf16[6,2,8,128,128]{4,3,2,1,0:T(8,128)(2,1)S(1)} copy-done((bf16[6,2,8,128,128]{4,3,2,1,0:T(8,128)(2,1)S(1)}, bf16[6,2,8,128,128]{4,3,2,1,0:T(8,128)(2,1)}, u32[]{:S(2)}) %copy-start.1) | copy-done | bytes 3145752
  3.8 0.0 copy-start.2
  3.8 1.6 copy-done.2
  5.4 0.0 copy-start.3
  5.4 0.7 copy-done.3
  6.0 181.0 %butterfly.1 = bf16[2,8,128,512]{3,2,1,0:T(8,128)(2,1)S(1)} custom-call(s32[32]{0:T(128)S(1)} %copy-done.3, bf16[32,8,8,512]{3,2,1,0:T(8,128)(2,1)S(1)} %bitcast.1, bf16[6,2,8,128,128]{4,3,2,1,0:T(8,128)(2,1)S(1)} %copy-done, bf16[6,2,8,128,128]{4,3,2,1,0:T(8,128)(2,1)S(1)} %copy-done.1), custom_call_target="tpu_custom_call" | custom-call | tf_op jit(solution)/shard_map/butterfly/pallas_call | solution.py:186
  187.0 1.3 copy.6
Async XLA Ops:
  0.0 1.9 %copy-start = (bf16[6,2,8,128,128]{4,3,2,1,0:T(8,128)(2,1)S(1)}, bf16[6,2,8,128,128]{4,3,2,1,0:T(8,128)(2,1)}, u32[]{:S(2)}) copy-start(bf16[6,2,8,128,128]{4,3,2,1,0:T(8,128)(2,1)} %self_ref.1) | copy-start | bytes 9437188
  1.9 1.9 %copy-start.1 = (bf16[6,2,8,128,128]{4,3,2,1,0:T(8,128)(2,1)S(1)}, bf16[6,2,8,128,128]{4,3,2,1,0:T(8,128)(2,1)}, u32[]{:S(2)}) copy-start(bf16[6,2,8,128,128]{4,3,2,1,0:T(8,128)(2,1)} %pair_ref.1) | copy-start | bytes 9437188
  3.8 1.6 copy-start.2
  5.4 0.7 copy-start.3

commit v2 on v1

--- a/solution.py
+++ b/solution.py
@@ -197,7 +197,7 @@
             dma((2, 2, n_level)), dma((2, 2)),
         ],
         compiler_params=pltpu.CompilerParams(
-            collective_id=0, has_side_effects=True, vmem_limit_bytes=40 << 20
+            collective_id=0, has_side_effects=True, vmem_limit_bytes=50 << 20
         ),
         name="butterfly",
     )(order_slot, fourier.reshape(orders, groups, rows, columns), coeff_self, coeff_pair)

time: 192 us -> 186 us (0.969)
  local copies, waits for them, and re-layouts: 7.34 us -> 1.98 us
    unnamed x9 -> x3, local copies, waits for them, and re-layouts: 7.34 us -> 1.98 us
where the time goes in v2:
time: 186 us; the launch traced here: 183 us
  Pallas kernels  181 us (97%)
  local copies, waits for them, and re-layouts  1.98 us (1%)
    pallas_call x1, Pallas kernels, local(): pl.pallas_call(functools.partial(kernel, n_order, n_level), out_shape=jax...  181 us

profile of v2, /device:TPU:1, one launch (start us, length us, event | category | flops | bytes accessed | tf_op | source)
XLA Modules:
  0.0 182.5 jit_solution(15014420623415707710)
XLA Ops:
  0.0 0.0 copy-start
  0.0 0.7 copy-done
  0.7 180.6 %butterfly.1 = bf16[2,8,128,512]{3,2,1,0:T(8,128)(2,1)S(1)} custom-call(s32[32]{0:T(128)S(1)} %copy-done, bf16[32,8,8,512]{3,2,1,0:T(8,128)(2,1)} %bitcast.1, bf16[6,2,8,128,128]{4,3,2,1,0:T(8,128)(2,1)} %self_ref.1, bf16[6,2,8,128,128]{4,3,2,1,0:T(8,128)(2,1)} %pair_ref.1), custom_call_target="tpu_custom_call" | custom-call | tf_op jit(solution)/shard_map/butterfly/pallas_call | solution.py:186
  181.2 1.3 copy.6
Async XLA Ops:
  0.0 0.7 copy-start

commit v3 on v2

--- a/solution.py
+++ b/solution.py
@@ -9,6 +9,8 @@
 
 MESH = pl.DeviceIdType.MESH
 CHUNKS = 2
+LEADER = 0
+HERALD = 1
 
 
 def mix(buf, c, coef, levels, slots, blocks):
@@ -38,7 +40,7 @@
 def kernel(
     n_order, n_level, slot_ref, fourier_ref, self_ref, pair_ref, out_ref,
     cycles, stage, by_cycle, blocks, turned, near, far,
-    load_sem, own_sem, z1_sem, xy_sem, z2_sem, z3_sem, coef_sem, core_sem,
+    joined, opened, load_sem, own_sem, z1_sem, xy_sem, z2_sem, z3_sem, coef_sem, core_sem,
 ):
     o, z, f = lax.axis_index("order"), lax.axis_index("level"), lax.axis_index("freq")
     chunks = stage.shape[0]
@@ -67,10 +69,43 @@
         copy.start()
 
     barrier = pltpu.get_barrier_semaphore()
-    loop(n_level, lambda d: pl.semaphore_signal(barrier, 1, device_id=(o, at_level(d), f), device_id_type=MESH))
-    loop(n_order, lambda d: pl.semaphore_signal(barrier, 1, device_id=(at_order(d), z, f), device_id_type=MESH))
+
+    def greet(d):
+        @pl.when(at_level(d) != LEADER)
+        def _():
+            pl.semaphore_signal(barrier, 1, device_id=(o, at_level(d), f), device_id_type=MESH)
+
+    loop(n_level, greet)
     pl.semaphore_signal(barrier, 1, device_id=(o, z, other), device_id_type=MESH)
-    pl.semaphore_wait(barrier, n_level + n_order - 1)
+
+    def enter():
+        @pl.when(z != LEADER)
+        def _():
+            pl.semaphore_wait(barrier, n_level)
+            pl.semaphore_signal(joined, 1, device_id=(o, LEADER, f), device_id_type=MESH)
+
+        @pl.when(z == LEADER)
+        def _():
+            pl.semaphore_wait(joined, n_level - 1)
+
+    def herald():
+        @pl.when(z == HERALD)
+        def _():
+            loop(n_order, lambda d: pl.semaphore_signal(
+                barrier, 1, device_id=(at_order(d), LEADER, f), device_id_type=MESH
+            ))
+
+    def meet_columns():
+        @pl.when(z == LEADER)
+        def _():
+            pl.semaphore_wait(barrier, n_order)
+            loop(n_level, lambda d: pl.semaphore_signal(
+                opened, 1, device_id=(o, at_level(d), f), device_id_type=MESH
+            ))
+
+        @pl.when(z != LEADER)
+        def _():
+            pl.semaphore_wait(opened, 1)
 
     def to_level(src, dst, sems, c, d):
         return pltpu.make_async_remote_copy(
@@ -132,7 +167,11 @@
             return carry
 
         lax.fori_loop(0, orders, place, 0)
+        if c == 0:
+            enter()
         loop(n_level, lambda d: z1(c, d).start())
+        if c == 0:
+            herald()
     for which in range(2):
         loop(n_level, lambda d: coef(which, d).start())
 
@@ -140,6 +179,8 @@
         copy.wait()
     for c in range(chunks):
         loop(n_level, lambda d: z1(c, d).wait_recv())
+        if c == 0:
+            meet_columns()
         loop(n_order, lambda d: xy(c, d).start())
         own["xy", c].start()
         own["xy", c].wait()
@@ -191,6 +232,7 @@
         scratch_shapes=[
             pltpu.VMEM((orders, groups, rows, columns), dtype),
             spread, spread, whole, whole, coefs, coefs,
+            pltpu.SemaphoreType.REGULAR, pltpu.SemaphoreType.REGULAR,
             dma((5,)), dma((3, CHUNKS)),
             dma((2, CHUNKS, n_level)), dma((2, CHUNKS, n_order)),
             dma((2, CHUNKS, n_level)), dma((2, CHUNKS, n_level)),

time: 186 us -> 182 us (0.978); the launches traced: 183 us -> 182 us
  no operation moved by 1% of the time
where the time goes in v3:
time: 182 us
  Pallas kernels  180 us (99%)
  local copies, waits for them, and re-layouts  1.98 us (1%)
    pallas_call x1, Pallas kernels, local(): pl.pallas_call(functools.partial(kernel, n_order, n_level), out_shape=jax...  180 us

profile of v3, /device:TPU:1, one launch (start us, length us, event | category | flops | bytes accessed | tf_op | source)
XLA Modules:
  0.0 182.2 jit_solution(14947197442309595396)
XLA Ops:
  0.0 0.0 copy-start
  0.0 0.7 copy-done
  0.7 180.2 %butterfly.1 = bf16[2,8,128,512]{3,2,1,0:T(8,128)(2,1)S(1)} custom-call(s32[32]{0:T(128)S(1)} %copy-done, bf16[32,8,8,512]{3,2,1,0:T(8,128)(2,1)} %bitcast.1, bf16[6,2,8,128,128]{4,3,2,1,0:T(8,128)(2,1)} %self_ref.1, bf16[6,2,8,128,128]{4,3,2,1,0:T(8,128)(2,1)} %pair_ref.1), custom_call_target="tpu_custom_call" | custom-call | tf_op jit(solution)/shard_map/butterfly/pallas_call | solution.py:227
  180.9 1.3 copy.6
Async XLA Ops:
  0.0 0.7 copy-start

commit v4 on v3

--- a/solution.py
+++ b/solution.py
@@ -9,7 +9,7 @@
 
 MESH = pl.DeviceIdType.MESH
 CHUNKS = 2
-LEADER = 0
+LEADER = 2
 HERALD = 1
 
 
@@ -58,6 +58,16 @@
     def loop(count, body):
         lax.fori_loop(1, count, lambda d, carry: (body(d), carry)[1], 0)
 
+    barrier = pltpu.get_barrier_semaphore()
+
+    def greet(d):
+        @pl.when(at_level(d) != LEADER)
+        def _():
+            pl.semaphore_signal(barrier, 1, device_id=(o, at_level(d), f), device_id_type=MESH)
+
+    loop(n_level, greet)
+    pl.semaphore_signal(barrier, 1, device_id=(o, z, other), device_id_type=MESH)
+
     loads = [
         pltpu.make_async_copy(fourier_ref, cycles, load_sem.at[0]),
         pltpu.make_async_copy(self_ref.at[pl.ds(0, levels)], near.at[0], load_sem.at[1]),
@@ -67,16 +77,6 @@
     ]
     for copy in loads:
         copy.start()
-
-    barrier = pltpu.get_barrier_semaphore()
-
-    def greet(d):
-        @pl.when(at_level(d) != LEADER)
-        def _():
-            pl.semaphore_signal(barrier, 1, device_id=(o, at_level(d), f), device_id_type=MESH)
-
-    loop(n_level, greet)
-    pl.semaphore_signal(barrier, 1, device_id=(o, z, other), device_id_type=MESH)
 
     def enter():
         @pl.when(z != LEADER)

time: 182 us -> 182 us (level)
  no operation moved by 1% of the time
where the time goes in v4:
time: 182 us
  Pallas kernels  180 us (99%)
  local copies, waits for them, and re-layouts  1.98 us (1%)
    pallas_call x1, Pallas kernels, local(): pl.pallas_call(functools.partial(kernel, n_order, n_level), out_shape=jax...  180 us

profile of v4, /device:TPU:1, one launch (start us, length us, event | category | flops | bytes accessed | tf_op | source)
XLA Modules:
  0.0 181.7 jit_solution(12776904809368422767)
XLA Ops:
  0.0 0.0 copy-start
  0.0 0.7 copy-done
  0.7 179.8 %butterfly.1 = bf16[2,8,128,512]{3,2,1,0:T(8,128)(2,1)S(1)} custom-call(s32[32]{0:T(128)S(1)} %copy-done, bf16[32,8,8,512]{3,2,1,0:T(8,128)(2,1)} %bitcast.1, bf16[6,2,8,128,128]{4,3,2,1,0:T(8,128)(2,1)} %self_ref.1, bf16[6,2,8,128,128]{4,3,2,1,0:T(8,128)(2,1)} %pair_ref.1), custom_call_target="tpu_custom_call" | custom-call | tf_op jit(solution)/shard_map/butterfly/pallas_call | solution.py:227
  180.4 1.3 copy.6
Async XLA Ops:
  0.0 0.7 copy-start
